TPU v7x, 32 devices: a whole 2x2x4 slice. The times are simulated.
32 devices in a mesh: groups: 2 (over x), tensor: 16 (over z, y, core).
Axes of the slice: x: 2, y: 2, z: 4, core: 2. Of those that a mesh axis runs over, the one named last changes fastest.
Arguments:
- teacher_in: bfloat16 [1024, 5376], P(('groups', 'tensor')), parts along dimension 0, may hold values from -6 to 6
- gate_weight: bfloat16 [21504, 5376], P('tensor'), may hold values from -0.078125 to 0.078125
- up_weight: bfloat16 [21504, 5376], P('tensor'), may hold values from -0.078125 to 0.078125
- down_weight: bfloat16 [21504, 5376], P('tensor'), may hold values from -0.0546875 to 0.0546875
- post_gain: bfloat16 [5376], replicated, may hold values from 0.099609375 to 1.8984375
- student_in: bfloat16 [1024, 2560], P(('groups', 'tensor')), parts along dimension 0, may hold values from -6 to 6
- proj_weight: bfloat16 [5376, 2560], P('tensor'), may hold values from -0.125 to 0.125
Outputs:
- loss_value: float32 [2], P('groups'), parts along dimension 0
- proj_grad: float32 [10752, 2560], P(('groups', 'tensor')), parts along dimension 0
- student_grad: bfloat16 [1024, 2560], P(('groups', 'tensor')), parts along dimension 0
There are 2 independent parts, one for each index of `groups`. A program takes and returns all parts, laid end to end along the dimension named above; an argument that names none is the same for every part. Nothing has to cross between parts.
All inputs are finite; a program needn't handle non-finite values.
Results may differ from a plain program's by a relative error of at most 0.0051.
Values may be sent and summed in bfloat16 or wider, within the bound.
A program may use at most 128 MiB of HBM per device.

v0:
```python
import jax
import jax.numpy as jnp
from jax import lax
from jax.sharding import PartitionSpec as P

epsilon = 1e-06


def local(teacher_in, gate_weight, up_weight, down_weight, post_gain, student_in, proj_weight):
    width_count = lax.axis_size("tensor")
    gains = post_gain.astype(jnp.float32)
    contract_last = (((1,), (1,)), ((), ()))
    block_rows = lax.all_gather(teacher_in, "tensor", axis=0, tiled=True)
    gate_value = lax.dot_general(
        block_rows, gate_weight, contract_last, preferred_element_type=jnp.float32
    )
    lift_value = lax.dot_general(
        block_rows, up_weight, contract_last, preferred_element_type=jnp.float32
    )
    hidden = (jax.nn.gelu(gate_value, approximate=True) * lift_value).astype(jnp.bfloat16)
    student_all = lax.all_gather(student_in, "tensor", axis=0, tiled=True)
    row_block = hidden
    ffn_out = lax.psum_scatter(
        jnp.dot(row_block, down_weight, preferred_element_type=jnp.float32),
        "tensor",
        scatter_dimension=0,
        tiled=True,
    )
    inv_norm = lax.rsqrt(jnp.mean(ffn_out * ffn_out, axis=-1, keepdims=True) + epsilon)
    target_rows = (teacher_in.astype(jnp.float32) + ffn_out * inv_norm * gains).astype(jnp.bfloat16)
    target = lax.all_to_all(target_rows, "tensor", split_axis=1, concat_axis=0, tiled=True)
    projected = lax.dot_general(
        student_all, proj_weight, contract_last, preferred_element_type=jnp.float32
    )
    difference = projected - target.astype(jnp.float32)
    total_error = lax.psum(jnp.sum(difference * difference), "tensor")
    loss_value = total_error / (student_all.shape[0] * proj_weight.shape[0] * width_count)
    cotangent = difference.astype(jnp.bfloat16)
    proj_grad = lax.dot_general(
        cotangent, student_all, (((0,), (0,)), ((), ())), preferred_element_type=jnp.float32
    )
    row_block = cotangent
    student_grad = lax.psum_scatter(
        jnp.dot(row_block, proj_weight, preferred_element_type=jnp.float32),
        "tensor",
        scatter_dimension=0,
        tiled=True,
    ).astype(jnp.bfloat16)
    return (jnp.reshape(loss_value, (1,)), proj_grad, student_grad)


def solution(mesh):
    placed = (
        P(("groups", "tensor"), None),
        P("tensor", None),
        P("tensor", None),
        P("tensor", None),
        P(),
        P(("groups", "tensor"), None),
        P("tensor", None),
    )
    return jax.shard_map(
        local,
        mesh=mesh,
        in_specs=placed,
        out_specs=(P("groups"), P(("groups", "tensor"), None), P(("groups", "tensor"), None)),
        check_vma=False,
    )
```

profile of v0, /device:TPU:0, one launch (start us, length us, event | category | flops | bytes accessed | tf_op | source)
XLA Modules:
  0.0 371.4 jit_solution(12804801437692001570)
XLA Ops:
  7.2 0.7 all-gather.5.cloned.1.call-update
  7.9 0.0 reduce-scatter.3.cloned.1.call-start
  8.0 62.5 %all-gather.5.cloned.1.call-done = bf16[512,5376]{1,0:T(8,128)(2,1)} async-done(((bf16[32,5376]{1,0:T(8,128)(2,1)}), bf16[512,5376]{1,0:T(8,128)(2,1)}) %all-gather.5.cloned.1.call-update) | async-done | bytes 5505040 | tf_op jit(solution)/shard_map/all_gather | solution.py:13
  70.4 13.7 %fusion.12 = f32[512,1344]{0,1:T(8,128)} fusion(bf16[512,5376]{1,0:T(8,128)(2,1)} %all-gather.5.cloned.1.call-done, bf16[1344,5376]{1,0:T(8,128)(2,1)} %param.8), kind=kOutput, calls=%fused_computation.19 | convolution fusion | flops 7398752256 | bytes 22708224 | tf_op jit(solution)/shard_map/dot_general | solution.py:14
  84.1 11.8 %fusion = bf16[512,1344]{0,1:T(8,128)(2,1)S(1)} fusion(bf16[512,5376]{1,0:T(8,128)(2,1)S(1)} %copy-done.3, bf16[1344,5376]{1,0:T(8,128)(2,1)} %param.9, f32[512,1344]{0,1:T(8,128)} %fusion.12), kind=kOutput, calls=%fused_computation.2 | convolution fusion | flops 7405633536 | bytes 24084480 | tf_op jit(solution)/shard_map/dot_general | solution.py:17
  96.0 11.5 %fusion.13 = f32[512,5376]{1,0:T(8,128)} fusion(bf16[512,1344]{0,1:T(8,128)(2,1)S(1)} %fusion, bf16[1344,5376]{1,0:T(8,128)(2,1)S(1)} %bitcast.18), kind=kOutput, calls=%fused_computation.20 | convolution fusion | flops 7398752256 | bytes 26836992 | tf_op jit(solution)/shard_map/dot_general | solution.py:24
  107.5 0.0 all-gather.3.cloned.1.call-start
  107.6 0.7 all-gather.3.cloned.1.call-update
  108.3 0.0 reduce-scatter.5.cloned.1.call-start
  108.4 120.6 %reduce-scatter.3.cloned.1.call-done = f32[32,5376]{1,0:T(8,128)} async-done(((f32[512,5376]{1,0:T(8,128)}), f32[32,5376]{1,0:T(8,128)}) %reduce-scatter.3.cloned.1.call-update) | async-done | bytes 688144 | tf_op jit(solution)/shard_map/reduce_scatter | solution.py:23
  229.0 1.3 multiply_reduce_fusion.1
  230.3 1.3 add_convert_fusion
  231.5 0.6 all_to_all.10
  232.1 0.1 copy.11
  232.2 20.2 %all_to_all.13 = bf16[32,16,336]{2,0,1:T(8,128)(2,1)S(1)} all-to-all(bf16[32,16,336]{2,0,1:T(8,128)(2,1)S(1)} %copy.11), channel_id=1, replica_groups=mesh['groups'=2,'tensor'=16] {'tensor'}, dimensions={1} | all-to-all | bytes 688128 | tf_op jit(solution)/shard_map/all_to_all | solution.py:31
  252.4 0.1 convert_element_type.37
  252.5 0.3 copy.12
  252.7 24.7 %all-gather.3.cloned.1.call-done = bf16[512,2560]{1,0:T(8,128)(2,1)} async-done(((bf16[32,2560]{1,0:T(8,128)(2,1)}), bf16[512,2560]{1,0:T(8,128)(2,1)}) %all-gather.3.cloned.1.call-update) | async-done | bytes 2621456 | tf_op jit(solution)/shard_map/all_gather | solution.py:21
  277.5 3.5 multiply_reduce_fusion
  281.0 3.8 %fusion.8 = f32[512,2560]{1,0:T(8,128)} fusion(bf16[336,2560]{1,0:T(8,128)(2,1)S(1)} %copy-done, bf16[512,336]{0,1:T(8,128)(2,1)S(1)} %get-tuple-element.4), kind=kOutput, calls=%fused_computation.14 | convolution fusion | flops 880803840 | bytes 7307264 | tf_op jit(solution)/shard_map/dot_general | solution.py:44
  284.9 32.1 %psum.7 = f32[]{:T(128)} all-reduce(f32[]{:T(128)} %get-tuple-element.3), channel_id=1, replica_groups=mesh['groups'=2,'tensor'=16] {'tensor'}, use_global_device_ids=true, to_apply=%region_3.0 | all-reduce | flops 1 | bytes 8 | tf_op jit(solution)/shard_map/psum | solution.py:36
  317.6 4.6 %fusion.10 = f32[336,2560]{1,0:T(8,128)} fusion(bf16[512,2560]{1,0:T(8,128)(2,1)} %all-gather.3.cloned.1.call-done, bf16[512,336]{0,1:T(8,128)(2,1)S(1)} %get-tuple-element.4), kind=kOutput, calls=%fused_computation.16 | convolution fusion | flops 880803840 | bytes 6406144 | tf_op jit(solution)/shard_map/dot_general | solution.py:39
  322.1 40.0 %reduce-scatter.5.cloned.1.call-done = f32[32,2560]{1,0:T(8,128)} async-done(((f32[512,2560]{1,0:T(8,128)}), f32[32,2560]{1,0:T(8,128)}) %reduce-scatter.5.cloned.1.call-update) | async-done | bytes 327696 | tf_op jit(solution)/shard_map/reduce_scatter | solution.py:43
  362.1 1.7 convert_element_type.35
  (22 shorter events, 0.1 us)
Async XLA Ops:
  7.2 270.3 %copy-start = (bf16[336,2560]{1,0:T(8,128)(2,1)S(1)}, bf16[336,2560]{1,0:T(8,128)(2,1)}, u32[]{:S(2)}) copy-start(bf16[336,2560]{1,0:T(8,128)(2,1)} %param.13) | copy-start | bytes 5160964
  7.2 63.2 %all-gather.5.cloned.1.call-start = ((), (), s32[]{:S(2)}) async-start(), calls=%async_computation.4 | async-start | bytes 5849088 | tf_op jit(solution)/shard_map/all_gather | solution.py:13
  7.9 221.1 %reduce-scatter.3.cloned.1.call-start = ((), (), s32[]{:S(2)}) async-start(), calls=%async_computation.5 | async-start | bytes 11698176 | tf_op jit(solution)/shard_map/reduce_scatter | solution.py:23
  70.4 13.7 %copy-start.3 = (bf16[512,5376]{1,0:T(8,128)(2,1)S(1)}, bf16[512,5376]{1,0:T(8,128)(2,1)}, u32[]{:S(2)}) copy-start(bf16[512,5376]{1,0:T(8,128)(2,1)} %all-gather.5.cloned.1.call-done) | copy-start | bytes 16515076
  70.4 25.6 %slice-start = ((s8[14450688]{0:T(1024)(128)(4,1)}), s8[4194304]{0:T(1024)(128)(4,1)S(1)}, s32[]{:S(2)}) async-start(s8[14450688]{0:T(1024)(128)(4,1)} %bitcast.17), calls=%async_computation.7 | async-start | bytes 8388608
  70.4 25.6 %slice-start.1 = ((s8[14450688]{0:T(1024)(128)(4,1)}), s8[4194304]{0:T(1024)(128)(4,1)S(1)}, s32[]{:S(2)}) async-start(s8[14450688]{0:T(1024)(128)(4,1)} %bitcast.17), calls=%async_computation.8 | async-start | bytes 8388608
  70.4 25.6 %slice-start.2 = ((s8[14450688]{0:T(1024)(128)(4,1)}), s8[4194304]{0:T(1024)(128)(4,1)S(1)}, s32[]{:S(2)}) async-start(s8[14450688]{0:T(1024)(128)(4,1)} %bitcast.17), calls=%async_computation.9 | async-start | bytes 8388608
  84.1 11.9 %slice-start.3 = ((s8[14450688]{0:T(1024)(128)(4,1)}), s8[1867776]{0:T(1024)(128)(4,1)S(1)}, s32[]{:S(2)}) async-start(s8[14450688]{0:T(1024)(128)(4,1)} %bitcast.17), calls=%async_computation.10 | async-start | bytes 3735552
  107.5 0.8 copy-start.2
  107.5 122.7 %copy-start.1 = (bf16[32,5376]{1,0:T(8,128)(2,1)S(1)}, bf16[32,5376]{1,0:T(8,128)(2,1)}, u32[]{:S(2)}) copy-start(bf16[32,5376]{1,0:T(8,128)(2,1)} %param.7) | copy-start | bytes 1032196
  107.5 169.9 %all-gather.3.cloned.1.call-start = ((), (), s32[]{:S(2)}) async-start(), calls=%async_computation.3 | async-start | bytes 2785280 | tf_op jit(solution)/shard_map/all_gather | solution.py:21
  108.3 253.8 %reduce-scatter.5.cloned.1.call-start = ((), (), s32[]{:S(2)}) async-start(), calls=%async_computation.6 | async-start | bytes 5570560 | tf_op jit(solution)/shard_map/reduce_scatter | solution.py:43
Sparse Core Ops, SparseCore 0:
  10.3 60.0 all-gather.4
  107.7 121.2 reduce-scatter.2
  231.5 45.8 all-gather.2
  285.0 77.0 reduce-scatter.4
where the time goes:
time: 372 us; the launch traced here: 371 us
  waiting for transfers between devices  249 us (67%)
  blocking collectives  52.2 us (14%)
  matrix products  48.9 us (13%)
  between operations  15.7 us (4%)
  other arithmetic  4.27 us (1%)
    reduce_scatter x1, waiting for transfers between devices, local(): lax.psum_scatter(jnp.dot(row_block, down_weight, preferred_element_type=j...  121 us
    all_gather x1, waiting for transfers between devices, local(): block_rows = lax.all_gather(teacher_in, 'tensor', axis=0, tiled=True)  62.5 us
    reduce_scatter x1, waiting for transfers between devices, local(): lax.psum_scatter(jnp.dot(row_block, proj_weight, preferred_element_type=j...  40 us
    psum x1, blocking collectives, local(): total_error = lax.psum(jnp.sum(difference * difference), 'tensor')  32.1 us
    all_gather x1, waiting for transfers between devices, local(): student_all = lax.all_gather(student_in, 'tensor', axis=0, tiled=True)  24.7 us
    all_to_all x1, blocking collectives, local(): lax.all_to_all(target_rows, 'tensor', split_axis=1, concat_axis=0, tiled=...  20.2 us
    dot_general x1, matrix products, local(): lax.dot_general(block_rows, gate_weight, contract_last, preferred_element...  13.7 us
    dot_general x1, matrix products, local(): lax.dot_general(block_rows, up_weight, contract_last, preferred_element_t...  11.8 us
  transfers between devices with their start and end apart: 4, of which 4 were waited for; matrix products, arithmetic and copies ran while one was open for 2% of the time, Pallas kernels for 0%

commit v1 on v0

v1 whole, which is shorter than its diff:
```python
import functools

import jax
import jax.numpy as jnp
from jax import lax
from jax.experimental import pallas as pl
from jax.experimental.pallas import tpu as pltpu
from jax.sharding import PartitionSpec as P

epsilon = 1e-06
MESH = pl.DeviceIdType.MESH


def send(src, dst, send_sem, recv_sem, target):
    return pltpu.make_async_remote_copy(
        src_ref=src,
        dst_ref=dst,
        send_sem=send_sem,
        recv_sem=recv_sem,
        device_id={"tensor": target},
        device_id_type=MESH,
    )


def meet(targets):
    barrier = pltpu.get_barrier_semaphore()
    for target in targets:
        pl.semaphore_signal(barrier, inc=1, device_id={"tensor": target}, device_id_type=MESH)
    pl.semaphore_wait(barrier, len(targets))


def position(Z):
    me = lax.axis_index("tensor")
    c = lax.rem(me, 2)
    y = lax.rem(me // 2, 2)
    z = me // 4
    core = me + 1 - 2 * c
    across = me + 2 - 4 * y
    line = [lax.rem(z + k, Z) for k in range(1, Z)]
    return me, c, y, z, core, across, line


def scatter_kernel(Z, J, n, sub, with_loss, *refs):
    if with_loss:
        (lhs, w, part, out, total, wbuf, p, r1, s1, r2, s2, r3, wsem,
         cs, cr, ys, yr, zs, zr, heard, hs, hr) = refs
    else:
        (lhs, w, out, wbuf, p, r1, s1, r2, s2, r3, wsem, cs, cr, ys, yr, zs, zr) = refs
    f32 = jnp.float32
    me, c, y, z, core, across, line = position(Z)
    T = 4 * Z
    B = out.shape[0]

    def fetch(j):
        return pltpu.make_async_copy(w.at[:, pl.ds(j * n, n)], wbuf.at[j % 2], wsem.at[j % 2])

    fetch(0).start()
    others = [lax.rem(me + k, T) for k in range(1, T)]
    meet(others if with_loss else [core, across] + [v * 4 + y * 2 + c for v in line])
    notes = []
    if with_loss:
        for k in range(T - 1):
            notes.append(send(part, heard.at[k], hs.at[k], hr.at[k], others[k]))
            notes[-1].start()

    first = [send(p.at[j, :, :, 1 - c], r1.at[j], cs.at[j], cr.at[j], core) for j in range(J)]
    second = [send(s1.at[j], r2.at[j], ys.at[j], yr.at[j], across) for j in range(J)]
    third = [
        [
            send(s2.at[j, v], r3.at[j, k], zs.at[j, k], zr.at[j, k], v * 4 + y * 2 + c)
            for k, v in enumerate(line)
        ]
        for j in range(J)
    ]

    for t in range(J + 3):
        if t < J:
            fetch(t).wait()
            if t + 1 < J:
                fetch(t + 1).start()

            @pl.loop(0, n // sub)
            def _(i, t=t):
                cols = pl.ds(pl.multiple_of(i * sub, sub), sub)
                got = jnp.dot(lhs[...], wbuf[t % 2, :, cols], preferred_element_type=f32)
                p[t, :, :, :, :, cols] = got.astype(jnp.bfloat16).reshape(Z, 2, 2, B, sub)

            first[t].start()
        j = t - 1
        if 0 <= j < J:
            first[j].wait_recv()
            s1[j] = (p[j, :, 1 - y, c].astype(f32) + r1[j, :, 1 - y].astype(f32)).astype(jnp.bfloat16)
            second[j].start()
        j = t - 2
        if 0 <= j < J:
            second[j].wait_recv()
            s2[j] = (
                p[j, :, y, c].astype(f32) + r1[j, :, y].astype(f32) + r2[j].astype(f32)
            ).astype(jnp.bfloat16)
            for copy in third[j]:
                copy.start()
        j = t - 3
        if 0 <= j < J:
            own = p[j, z, y, c].astype(f32) + r1[j, z, y].astype(f32) + r2[j, z].astype(f32)
            for k, copy in enumerate(third[j]):
                copy.wait_recv()
                own += r3[j, k].astype(f32)
            out[:, j * n : (j + 1) * n] = own.astype(out.dtype)
    for j in range(J):
        first[j].wait_send()
        second[j].wait_send()
        for copy in third[j]:
            copy.wait_send()
    if with_loss:
        acc = part[...]
        for k, copy in enumerate(notes):
            copy.wait()
            acc += heard[k]
        total[...] = acc


def scatter_matmul(lhs, w, T, n, sub, dtype, name, cid, part=None):
    Z = T // 4
    rows, K = lhs.shape
    N = w.shape[1]
    J, B = N // n, rows // T
    bf = jnp.bfloat16
    V = pltpu.VMEM
    D = pltpu.SemaphoreType.DMA
    vm = pl.BlockSpec(memory_space=pltpu.VMEM)
    with_loss = part is not None
    scratch = [
        V((2, K, n), bf), V((J, Z, 2, 2, B, n), bf), V((J, Z, 2, B, n), bf), V((J, Z, B, n), bf),
        V((J, Z, B, n), bf), V((J, Z, B, n), bf), V((J, Z - 1, B, n), bf), D((2,)),
        D((J,)), D((J,)), D((J,)), D((J,)), D((J, Z - 1)), D((J, Z - 1)),
    ]
    outs = [jax.ShapeDtypeStruct((B, N), dtype)]
    args = [lhs, w]
    specs = [vm, pl.BlockSpec(memory_space=pl.ANY)]
    if with_loss:
        scratch += [V((T - 1, 8, 128), jnp.float32), D((T - 1,)), D((T - 1,))]
        outs.append(jax.ShapeDtypeStruct((8, 128), jnp.float32))
        args.append(part)
        specs.append(vm)
    return pl.pallas_call(
        functools.partial(scatter_kernel, Z, J, n, sub, with_loss),
        out_shape=outs,
        in_specs=specs,
        out_specs=[vm] * len(outs),
        scratch_shapes=scratch,
        name=name,
        cost_estimate=pl.CostEstimate(
            flops=2 * rows * K * N, bytes_accessed=2 * (K * N + rows * K), transcendentals=0
        ),
        compiler_params=pltpu.CompilerParams(
            collective_id=cid, has_side_effects=True, vmem_limit_bytes=48 * 2**20
        ),
    )(*args)


def local(teacher_in, gate_weight, up_weight, down_weight, post_gain, student_in, proj_weight):
    width_count = lax.axis_size("tensor")
    own_sums = width_count == 16 and teacher_in.shape[0] % 16 == 0
    gains = post_gain.astype(jnp.float32)
    contract_last = (((1,), (1,)), ((), ()))
    block_rows = lax.all_gather(teacher_in, "tensor", axis=0, tiled=True)
    gate_value = lax.dot_general(
        block_rows, gate_weight, contract_last, preferred_element_type=jnp.float32
    )
    lift_value = lax.dot_general(
        block_rows, up_weight, contract_last, preferred_element_type=jnp.float32
    )
    hidden = (jax.nn.gelu(gate_value, approximate=True) * lift_value).astype(jnp.bfloat16)
    student_all = lax.all_gather(student_in, "tensor", axis=0, tiled=True)
    if own_sums:
        (ffn_out,) = scatter_matmul(
            hidden, down_weight, width_count, 768, 256, jnp.float32, "down_scatter", 1
        )
    else:
        ffn_out = lax.psum_scatter(
            jnp.dot(hidden, down_weight, preferred_element_type=jnp.float32),
            "tensor",
            scatter_dimension=0,
            tiled=True,
        )
    inv_norm = lax.rsqrt(jnp.mean(ffn_out * ffn_out, axis=-1, keepdims=True) + epsilon)
    target_rows = (teacher_in.astype(jnp.float32) + ffn_out * inv_norm * gains).astype(jnp.bfloat16)
    target = lax.all_to_all(target_rows, "tensor", split_axis=1, concat_axis=0, tiled=True)
    projected = lax.dot_general(
        student_all, proj_weight, contract_last, preferred_element_type=jnp.float32
    )
    difference = projected - target.astype(jnp.float32)
    squares = jnp.sum(difference * difference)
    cotangent = difference.astype(jnp.bfloat16)
    proj_grad = lax.dot_general(
        cotangent, student_all, (((0,), (0,)), ((), ())), preferred_element_type=jnp.float32
    )
    if own_sums:
        student_grad, total = scatter_matmul(
            cotangent, proj_weight, width_count, 512, 256, jnp.bfloat16, "grad_scatter", 2,
            jnp.full((8, 128), squares, jnp.float32),
        )
        total_error = total[0, 0]
    else:
        total_error = lax.psum(squares, "tensor")
        student_grad = lax.psum_scatter(
            jnp.dot(cotangent, proj_weight, preferred_element_type=jnp.float32),
            "tensor",
            scatter_dimension=0,
            tiled=True,
        ).astype(jnp.bfloat16)
    loss_value = total_error / (student_all.shape[0] * proj_weight.shape[0] * width_count)
    return (jnp.reshape(loss_value, (1,)), proj_grad, student_grad)


def solution(mesh):
    placed = (
        P(("groups", "tensor"), None),
        P("tensor", None),
        P("tensor", None),
        P("tensor", None),
        P(),
        P(("groups", "tensor"), None),
        P("tensor", None),
    )
    return jax.shard_map(
        local,
        mesh=mesh,
        in_specs=placed,
        out_specs=(P("groups"), P(("groups", "tensor"), None), P(("groups", "tensor"), None)),
        check_vma=False,
    )
```

time: 372 us -> 212 us (0.57)
  waiting for transfers between devices: 249 us -> 62.4 us
  Pallas kernels: 0 us -> 71.5 us
  blocking collectives: 52.2 us -> 16.1 us
  matrix products: 48.9 us -> 36.6 us
  local copies, waits for them, and re-layouts: 0.94 us -> 8.23 us
    reduce_scatter x2 -> x0, waiting for transfers between devices: 161 us -> none  [the longest x1 121 us: local(): lax.psum_scatter(jnp.dot(row_block, down_weight, preferred_element_type=j...]
    pallas_call x0 -> x2, Pallas kernels: none -> 71.5 us  [scatter_matmul(): pl.pallas_call(functools.partial(scatter_kernel, Z, J, n, sub, with_loss)...]
    psum x1 -> x0, blocking collectives: 32.1 us -> none  [local(): total_error = lax.psum(jnp.sum(difference * difference), 'tensor')]
    all_gather x1, waiting for transfers between devices: 24.7 us -> 0.02 us  [local(): student_all = lax.all_gather(student_in, 'tensor', axis=0, tiled=True)]
    dot_general x2 -> x0, matrix products: 15.3 us -> none  [the longest x1 11.5 us: local(): jnp.dot(row_block, down_weight, preferred_element_type=jnp.float32)]
    dot_general x1, matrix products: 11.8 us -> 16.2 us  [local(): lax.dot_general(block_rows, up_weight, contract_last, preferred_element_t...]
    all_to_all x1, blocking collectives: 20.2 us -> 16.1 us  [local(): lax.all_to_all(target_rows, 'tensor', split_axis=1, concat_axis=0, tiled=...]
  transfers between devices with their start and end apart: 4 -> 2, of which waited for: 4 -> 1; matrix products, arithmetic and copies ran while one was open for 2% -> 17% of each run, Pallas kernels for 0% -> 21%
where the time goes in v1:
time: 212 us
  Pallas kernels  71.5 us (34%)
  waiting for transfers between devices  62.4 us (29%)
  matrix products  36.6 us (17%)
  blocking collectives  16.1 us (8%)
  between operations  15.9 us (8%)
  local copies, waits for them, and re-layouts  8.23 us (4%)
    pallas_call x2, Pallas kernels, scatter_matmul(): pl.pallas_call(functools.partial(scatter_kernel, Z, J, n, sub, with_loss)...  71.5 us
    all_gather x1, waiting for transfers between devices, local(): block_rows = lax.all_gather(teacher_in, 'tensor', axis=0, tiled=True)  61 us
    dot_general x1, matrix products, local(): lax.dot_general(block_rows, up_weight, contract_last, preferred_element_t...  16.2 us
    all_to_all x1, blocking collectives, local(): lax.all_to_all(target_rows, 'tensor', split_axis=1, concat_axis=0, tiled=...  16.1 us
    dot_general x1, matrix products, local(): lax.dot_general(block_rows, gate_weight, contract_last, preferred_element...  13.6 us
  transfers between devices with their start and end apart: 2, of which 1 were waited for; matrix products, arithmetic and copies ran while one was open for 17% of the time, Pallas kernels for 21%

profile of v1, /device:TPU:0, one launch (start us, length us, event | category | flops | bytes accessed | tf_op | source)
XLA Modules:
  0.0 212.0 jit_solution(8444246602512003848)
XLA Ops:
  7.2 0.0 all-gather.5.cloned.1.call-start
  7.2 0.7 all-gather.5.cloned.1.call-update
  7.9 0.0 all-gather.3.cloned.1.call-start
  7.9 0.7 all-gather.3.cloned.1.call-update
  8.6 0.7 convert_element_type.26
  9.4 61.0 %all-gather.5.cloned.1.call-done = bf16[512,5376]{1,0:T(8,128)(2,1)} async-done(((bf16[32,5376]{1,0:T(8,128)(2,1)}), bf16[512,5376]{1,0:T(8,128)(2,1)}) %all-gather.5.cloned.1.call-update) | async-done | bytes 5505040 | tf_op jit(solution)/shard_map/all_gather | solution.py:166
  70.4 13.6 %fusion.1 = (f32[512,1344]{0,1:T(8,128)}, f32[512,1344]{0,1:T(8,128)S(1)}) fusion(bf16[512,5376]{1,0:T(8,128)(2,1)} %all-gather.5.cloned.1.call-done, bf16[1344,5376]{1,0:T(8,128)(2,1)} %param.8), kind=kOutput, calls=%fused_computation.7 | convolution fusion | flops 7399440384 | bytes 25460736 | tf_op jit(solution)/shard_map/dot_general | solution.py:167
  84.0 3.4 %copy.18 = f32[512,1344]{1,0:T(8,128)} copy(f32[512,1344]{0,1:T(8,128)} %get-tuple-element.9) | data formatting | bytes 5505024 | tf_op jit(solution)/shard_map/integer_pow | solution.py:173
  87.4 2.2 %copy.21 = f32[512,1344]{1,0:T(8,128)} copy(f32[512,1344]{0,1:T(8,128)S(1)} %get-tuple-element.10) | data formatting | bytes 5505024 | tf_op jit(solution)/shard_map/dot_general | solution.py:167
  89.6 16.2 %fusion.refs_0_ = bf16[512,1344]{1,0:T(8,128)(2,1)S(1)} fusion(bf16[512,5376]{1,0:T(8,128)(2,1)} %all-gather.5.cloned.1.call-done, bf16[1344,5376]{1,0:T(8,128)(2,1)} %param.9, f32[512,1344]{1,0:T(8,128)} %copy.21, f32[512,1344]{1,0:T(8,128)} %copy.18), kind=kOutput, calls=%fused_computation.1 | convolution fusion | flops 7404945408 | bytes 26836992 | tf_op jit(solution)/shard_map/dot_general | solution.py:170
  105.8 44.7 %down_scatter.1 = f32[32,5376]{1,0:T(8,128)S(1)} custom-call(bf16[512,1344]{1,0:T(8,128)(2,1)S(1)} %fusion.refs_0_, bf16[1344,5376]{1,0:T(8,128)(2,1)} %refs_1_.2), custom_call_target="tpu_custom_call" | custom-call | flops 7398752256 | bytes 15826944 | tf_op jit(solution)/shard_map/down_scatter/pallas_call | solution.py:145
  150.5 0.2 multiply_reduce_fusion.1
  150.7 0.2 add_convert_fusion
  150.9 0.6 all_to_all.10
  151.5 0.1 copy.23
  151.6 16.1 %all_to_all.13 = bf16[32,16,336]{2,0,1:T(8,128)(2,1)S(1)} all-to-all(bf16[32,16,336]{2,0,1:T(8,128)(2,1)S(1)} %copy.23), channel_id=1, replica_groups=mesh['groups'=2,'tensor'=16] {'tensor'}, dimensions={1} | all-to-all | bytes 688128 | tf_op jit(solution)/shard_map/all_to_all | solution.py:188
  167.7 0.1 convert_element_type.33
  167.7 0.0 all-gather.3.cloned.1.call-done
  167.8 4.0 %multiply_reduce_fusion = (f32[]{:T(128)}, bf16[512,336]{1,0:T(8,128)(2,1)S(1)}) fusion(f32[512,336]{1,0:T(8,128)S(1)} %bitcast.12, bf16[512,2560]{1,0:T(8,128)(2,1)} %all-gather.3.cloned.1.call-done, bf16[336,2560]{1,0:T(8,128)(2,1)S(1)} %copy-done), kind=kOutput, calls=%fused_computation.3 | convolution fusion | flops 881491968 | bytes 5373956 | tf_op jit(solution)/shard_map/dot_general | solution.py:189
  171.7 0.8 broadcast_in_dim.2.refs_2_
  172.5 26.8 %grad_scatter.1 = (bf16[32,2560]{1,0:T(8,128)(2,1)S(1)}, f32[8,128]{1,0:T(8,128)S(1)}) custom-call(bf16[512,336]{1,0:T(8,128)(2,1)S(1)} %get-tuple-element.8.refs_0_, bf16[336,2560]{1,0:T(8,128)(2,1)S(1)} %copy-done, f32[8,128]{1,0:T(8,128)S(1)} %broadcast_in_dim.2.refs_2_), custom_call_target="tpu_custom_call" | custom-call | flops 880803840 | bytes 2064384 | tf_op jit(solution)/shard_map/grad_scatter/pallas_call | solution.py:145
  199.3 0.5 slice.3
  200.5 2.8 %fusion.2 = f32[336,2560]{1,0:T(8,128)} fusion(bf16[512,336]{1,0:T(8,128)(2,1)S(1)} %get-tuple-element.8.refs_0_, bf16[512,2560]{1,0:T(8,128)(2,1)S(1)} %copy-done.1), kind=kOutput, calls=%fused_computation.8 | convolution fusion | flops 880803840 | bytes 6406144 | tf_op jit(solution)/shard_map/dot_general | solution.py:195
  203.3 0.7 copy.28
  (7 shorter events, 0.0 us)
Async XLA Ops:
  7.2 63.2 %all-gather.5.cloned.1.call-start = ((), (), s32[]{:S(2)}) async-start(), calls=%async_computation.2 | async-start | bytes 5849088 | tf_op jit(solution)/shard_map/all_gather | solution.py:166
  7.9 159.9 %all-gather.3.cloned.1.call-start = ((), (), s32[]{:S(2)}) async-start(), calls=%async_computation.1 | async-start | bytes 2785280 | tf_op jit(solution)/shard_map/all_gather | solution.py:174
  105.8 45.0 %copy-start.2 = (bf16[32,5376]{1,0:T(8,128)(2,1)S(1)}, bf16[32,5376]{1,0:T(8,128)(2,1)}, u32[]{:S(2)}) copy-start(bf16[32,5376]{1,0:T(8,128)(2,1)} %param.7) | copy-start | bytes 1032196
  150.5 17.2 %copy-start = (bf16[336,2560]{1,0:T(8,128)(2,1)S(1)}, bf16[336,2560]{1,0:T(8,128)(2,1)}, u32[]{:S(2)}) copy-start(bf16[336,2560]{1,0:T(8,128)(2,1)} %refs_1_.3) | copy-start | bytes 5160964
  171.7 28.8 %copy-start.1 = (bf16[512,2560]{1,0:T(8,128)(2,1)S(1)}, bf16[512,2560]{1,0:T(8,128)(2,1)}, u32[]{:S(2)}) copy-start(bf16[512,2560]{1,0:T(8,128)(2,1)} %all-gather.3.cloned.1.call-done) | copy-start | bytes 7864324
Sparse Core Ops, SparseCore 0:
  10.3 60.0 all-gather.4
  72.7 42.0 all-gather.2

commit v2 on v1

--- a/solution.py
+++ b/solution.py
@@ -82,7 +82,14 @@
             @pl.loop(0, n // sub)
             def _(i, t=t):
                 cols = pl.ds(pl.multiple_of(i * sub, sub), sub)
-                got = jnp.dot(lhs[...], wbuf[t % 2, :, cols], preferred_element_type=f32)
+                depth = lhs.shape[2]
+                got = sum(
+                    jnp.dot(
+                        lhs[q], wbuf[t % 2, q * depth : (q + 1) * depth, cols],
+                        preferred_element_type=f32,
+                    )
+                    for q in range(lhs.shape[0])
+                )
                 p[t, :, :, :, :, cols] = got.astype(jnp.bfloat16).reshape(Z, 2, 2, B, sub)
 
             first[t].start()
@@ -119,10 +126,136 @@
         total[...] = acc
 
 
+def gather_kernel(Z, J, n, S, m, G, x, st, gate, up, hidden, student, wbuf, xa, xs, acc,
+                  wsem, zs, zr, ys, yr, cs, cr):
+    f32 = jnp.float32
+    me, c, y, z, core, across, line = position(Z)
+    B = x.shape[0]
+    R = 4 * Z * B
+    g = gate.shape[0] // G
+
+    def fetch(j):
+        cols = pl.ds(j * n, n)
+        return [
+            pltpu.make_async_copy(w.at[:, cols], wbuf.at[i, j % 2], wsem.at[i, j % 2])
+            for i, w in enumerate((gate, up))
+        ]
+
+    for j in range(min(2, J)):
+        for copy in fetch(j):
+            copy.start()
+    for j in range(J):
+        xa[j, z, y, c] = x[:, j * n : (j + 1) * n]
+    for j in range(S):
+        xs[j, z, y, c] = st[:, j * m : (j + 1) * m]
+    targets = [v * 4 + y * 2 + c for v in line]
+    meet([core, across] + targets)
+
+    items = [xa.at[j] for j in range(J)] + [xs.at[j] for j in range(S)]
+    first = [
+        [
+            send(a.at[z, y, c], a.at[z, y, c], zs.at[i, k], zr.at[i, k], v)
+            for k, v in enumerate(targets)
+        ]
+        for i, a in enumerate(items)
+    ]
+    second = [
+        send(a.at[:, y, c], a.at[:, y, c], ys.at[i], yr.at[i], across)
+        for i, a in enumerate(items)
+    ]
+    third = [
+        send(a.at[:, :, c], a.at[:, :, c], cs.at[i], cr.at[i], core)
+        for i, a in enumerate(items)
+    ]
+
+    def multiply(j):
+        for copy in fetch(j):
+            copy.wait()
+
+        @pl.loop(0, G)
+        def _(i):
+            rows = pl.ds(pl.multiple_of(i * g, 16), g)
+            block = xa[j].reshape(R, n)
+            got = []
+            for which in range(2):
+                d = lax.dot_general(
+                    block, wbuf[which, j % 2, rows, :], (((1,), (1,)), ((), ())),
+                    preferred_element_type=f32,
+                )
+                if j > 0:
+                    d += acc[which, i]
+                if j < J - 1:
+                    acc[which, i] = d
+                got.append(d)
+            if j == J - 1:
+                hidden[i] = (jax.nn.gelu(got[0], approximate=True) * got[1]).astype(jnp.bfloat16)
+
+        if j + 2 < J:
+            for copy in fetch(j + 2):
+                copy.start()
+
+    for t in range(J + S + 3):
+        if t < J + S:
+            for copy in first[t]:
+                copy.start()
+        if 0 <= t - 1 < J + S:
+            for copy in first[t - 1]:
+                copy.wait_recv()
+            second[t - 1].start()
+        if 0 <= t - 2 < J + S:
+            second[t - 2].wait_recv()
+            third[t - 2].start()
+        if 0 <= t - 3 < J + S:
+            third[t - 3].wait_recv()
+            if t - 3 < J:
+                multiply(t - 3)
+            else:
+                j = t - 3 - J
+                student[:, j * m : (j + 1) * m] = xs[j].reshape(R, m)
+    for i in range(J + S):
+        for copy in first[i]:
+            copy.wait_send()
+        second[i].wait_send()
+        third[i].wait_send()
+
+
+def gather_ffn(x, st, gate, up, T, n, m, G, cid):
+    Z = T // 4
+    B, K = x.shape
+    N = gate.shape[0]
+    J, S = K // n, st.shape[1] // m
+    bf = jnp.bfloat16
+    V = pltpu.VMEM
+    D = pltpu.SemaphoreType.DMA
+    vm = pl.BlockSpec(memory_space=pltpu.VMEM)
+    hbm = pl.BlockSpec(memory_space=pl.ANY)
+    return pl.pallas_call(
+        functools.partial(gather_kernel, Z, J, n, S, m, G),
+        out_shape=[
+            jax.ShapeDtypeStruct((G, T * B, N // G), bf),
+            jax.ShapeDtypeStruct((T * B, st.shape[1]), bf),
+        ],
+        in_specs=[vm, vm, hbm, hbm],
+        out_specs=[vm, vm],
+        scratch_shapes=[
+            V((2, 2, N, n), bf), V((J, Z, 2, 2, B, n), bf), V((S, Z, 2, 2, B, m), bf),
+            V((2, G, T * B, N // G), jnp.float32), D((2, 2)),
+            D((J + S, Z - 1)), D((J + S, Z - 1)), D((J + S,)), D((J + S,)), D((J + S,)), D((J + S,)),
+        ],
+        name="gather_ffn",
+        cost_estimate=pl.CostEstimate(
+            flops=4 * T * B * K * N, bytes_accessed=4 * K * N, transcendentals=0
+        ),
+        compiler_params=pltpu.CompilerParams(
+            collective_id=cid, has_side_effects=True, vmem_limit_bytes=48 * 2**20
+        ),
+    )(x, st, gate, up)
+
+
 def scatter_matmul(lhs, w, T, n, sub, dtype, name, cid, part=None):
     Z = T // 4
-    rows, K = lhs.shape
-    N = w.shape[1]
+    rows = lhs.shape[1]
+    K, N = w.shape
     J, B = N // n, rows // T
     bf = jnp.bfloat16
     V = pltpu.VMEM
@@ -163,15 +296,20 @@
     own_sums = width_count == 16 and teacher_in.shape[0] % 16 == 0
     gains = post_gain.astype(jnp.float32)
     contract_last = (((1,), (1,)), ((), ()))
-    block_rows = lax.all_gather(teacher_in, "tensor", axis=0, tiled=True)
-    gate_value = lax.dot_general(
-        block_rows, gate_weight, contract_last, preferred_element_type=jnp.float32
-    )
-    lift_value = lax.dot_general(
-        block_rows, up_weight, contract_last, preferred_element_type=jnp.float32
-    )
-    hidden = (jax.nn.gelu(gate_value, approximate=True) * lift_value).astype(jnp.bfloat16)
-    student_all = lax.all_gather(student_in, "tensor", axis=0, tiled=True)
+    if own_sums:
+        hidden, student_all = gather_ffn(
+            teacher_in, student_in, gate_weight, up_weight, width_count, 768, 640, 6, 3
+        )
+    else:
+        block_rows = lax.all_gather(teacher_in, "tensor", axis=0, tiled=True)
+        gate_value = lax.dot_general(
+            block_rows, gate_weight, contract_last, preferred_element_type=jnp.float32
+        )
+        lift_value = lax.dot_general(
+            block_rows, up_weight, contract_last, preferred_element_type=jnp.float32
+        )
+        hidden = (jax.nn.gelu(gate_value, approximate=True) * lift_value).astype(jnp.bfloat16)
+        student_all = lax.all_gather(student_in, "tensor", axis=0, tiled=True)
     if own_sums:
         (ffn_out,) = scatter_matmul(
             hidden, down_weight, width_count, 768, 256, jnp.float32, "down_scatter", 1
@@ -197,7 +335,7 @@
     )
     if own_sums:
         student_grad, total = scatter_matmul(
-            cotangent, proj_weight, width_count, 512, 256, jnp.bfloat16, "grad_scatter", 2,
+            cotangent[None], proj_weight, width_count, 512, 256, jnp.bfloat16, "grad_scatter", 2,
             jnp.full((8, 128), squares, jnp.float32),
         )
         total_error = total[0, 0]

time: 212 us -> 172 us (0.81)
  Pallas kernels: 71.5 us -> 140 us
  waiting for transfers between devices: 62.4 us -> 0 us
  matrix products: 36.6 us -> 4.37 us
  between operations: 15.9 us -> 2.51 us
  local copies, waits for them, and re-layouts: 8.23 us -> 4.39 us
    pallas_call x0 -> x1, Pallas kernels: none -> 69.8 us  [gather_ffn(): pl.pallas_call(functools.partial(gather_kernel, Z, J, n, S, m, G), out_sh...]
    all_gather x2 -> x0, waiting for transfers between devices: 61.1 us -> none  [the longest x1 61 us: local(): block_rows = lax.all_gather(teacher_in, 'tensor', axis=0, tiled=True)]
    dot_general x2 -> x0, matrix products: 29.8 us -> none  [the longest x1 16.2 us: local(): lax.dot_general(block_rows, up_weight, contract_last, preferred_element_t...]
    integer_pow x1 -> x0, local copies, waits for them, and re-layouts: 3.38 us -> none  [local(): jax.nn.gelu(gate_value, approximate=True) * lift_value]
    dot_general x1, matrix products: 3.95 us -> 1.53 us  [local(): lax.dot_general(student_all, proj_weight, contract_last, preferred_elemen...]
    dot_general x1 -> x0, local copies, waits for them, and re-layouts: 2.21 us -> none  [local(): lax.dot_general(block_rows, gate_weight, contract_last, preferred_element...]
  transfers between devices with their start and end apart: 2 -> 0, of which waited for: 1 -> 0; matrix products, arithmetic and copies ran while one was open for 17% -> 0% of each run, Pallas kernels for 21% -> 0%
where the time goes in v2:
time: 172 us; the launch traced here: 171 us
  Pallas kernels  140 us (81%)
  blocking collectives  17.7 us (10%)
  local copies, waits for them, and re-layouts  4.39 us (3%)
  matrix products  4.37 us (3%)
  between operations  2.51 us (1%)
  other arithmetic  1.94 us (1%)
    pallas_call x2, Pallas kernels, scatter_matmul(): pl.pallas_call(functools.partial(scatter_kernel, Z, J, n, sub, with_loss)...  70.6 us
    pallas_call x1, Pallas kernels, gather_ffn(): pl.pallas_call(functools.partial(gather_kernel, Z, J, n, S, m, G), out_sh...  69.8 us
    all_to_all x1, blocking collectives, local(): lax.all_to_all(target_rows, 'tensor', split_axis=1, concat_axis=0, tiled=...  17.7 us

profile of v2, /device:TPU:0, one launch (start us, length us, event | category | flops | bytes accessed | tf_op | source)
XLA Modules:
  0.0 171.2 jit_solution(15680307235545012834)
XLA Ops:
  0.6 0.7 convert_element_type.22
  1.3 0.0 copy-start
  1.3 1.0 copy-done
  2.3 0.0 copy-start.3
  2.3 0.9 copy-done.3
  3.2 69.8 %gather_ffn.1 = (bf16[6,512,224]{2,1,0:T(8,128)(2,1)S(1)}, bf16[512,2560]{1,0:T(8,128)(2,1)S(1)}) custom-call(bf16[32,5376]{1,0:T(8,128)(2,1)S(1)} %copy-done, bf16[32,2560]{1,0:T(8,128)(2,1)S(1)} %copy-done.3, bf16[1344,5376]{1,0:T(8,128)(2,1)} %gate.1, bf16[1344,5376]{1,0:T(8,128)(2,1)} %up.1), custom_call_target="tpu_custom_call" | custom-call | flops 14797504512 | bytes 28901376 | tf_op jit(solution)/shard_map/gather_ffn/pallas_call | solution.py:232
  73.0 0.0 copy-start.1
  73.0 43.8 %down_scatter.1 = f32[32,5376]{1,0:T(8,128)S(1)} custom-call(bf16[6,512,224]{2,1,0:T(8,128)(2,1)S(1)} %get-tuple-element.8.refs_0_, bf16[1344,5376]{1,0:T(8,128)(2,1)} %refs_1_.2), custom_call_target="tpu_custom_call" | custom-call | flops 7398752256 | bytes 15826944 | tf_op jit(solution)/shard_map/down_scatter/pallas_call | solution.py:278
  116.8 0.2 multiply_reduce_fusion.1
  117.0 0.0 copy-done.1
  117.0 0.2 add_convert_fusion
  117.2 0.6 all_to_all.10
  117.8 0.0 copy-start.2
  117.8 0.1 copy.10
  117.9 17.7 %all_to_all.13 = bf16[32,16,336]{2,0,1:T(8,128)(2,1)S(1)} all-to-all(bf16[32,16,336]{2,0,1:T(8,128)(2,1)S(1)} %copy.10), channel_id=1, replica_groups=mesh['groups'=2,'tensor'=16] {'tensor'}, dimensions={1} | all-to-all | bytes 688128 | tf_op jit(solution)/shard_map/all_to_all | solution.py:326
  135.5 0.1 convert_element_type.29
  135.6 0.0 copy-done.2
  135.6 1.5 convolution_subtract_fusion
  137.2 0.8 multiply_reduce_fusion
  138.0 2.8 %fusion = f32[336,2560]{1,0:T(8,128)} fusion(bf16[512,2560]{1,0:T(8,128)(2,1)S(1)} %get-tuple-element.7, f32[512,336]{1,0:T(8,128)S(1)} %convolution_subtract_fusion), kind=kOutput, calls=%fused_computation.4 | convolution fusion | flops 880975872 | bytes 6750208 | tf_op jit(solution)/shard_map/dot_general | solution.py:333
  140.8 0.6 broadcast_in_dim.9.refs_2_
  141.5 26.8 %grad_scatter.1 = (bf16[32,2560]{1,0:T(8,128)(2,1)S(1)}, f32[8,128]{1,0:T(8,128)S(1)}) custom-call(bf16[1,512,336]{2,1,0:T(8,128)(2,1)S(1)} %get-tuple-element.12.refs_0_, bf16[336,2560]{1,0:T(8,128)(2,1)S(1)} %copy-done.2, f32[8,128]{1,0:T(8,128)S(1)} %broadcast_in_dim.9.refs_2_), custom_call_target="tpu_custom_call" | custom-call | flops 880803840 | bytes 2064384 | tf_op jit(solution)/shard_map/grad_scatter/pallas_call | solution.py:278
  168.3 0.5 slice.3
  169.4 0.7 copy.14
  (1 shorter events, 0.0 us)
Async XLA Ops:
  1.3 1.0 copy-start
  2.3 0.9 copy-start.3
  73.0 44.0 %copy-start.1 = (bf16[32,5376]{1,0:T(8,128)(2,1)S(1)}, bf16[32,5376]{1,0:T(8,128)(2,1)}, u32[]{:S(2)}) copy-start(bf16[32,5376]{1,0:T(8,128)(2,1)} %x.1) | copy-start | bytes 1032196
  117.8 17.8 %copy-start.2 = (bf16[336,2560]{1,0:T(8,128)(2,1)S(1)}, bf16[336,2560]{1,0:T(8,128)(2,1)}, u32[]{:S(2)}) copy-start(bf16[336,2560]{1,0:T(8,128)(2,1)} %refs_1_.3) | copy-start | bytes 5160964

commit v3 on v2

--- a/solution.py
+++ b/solution.py
@@ -8,6 +8,7 @@
 from jax.sharding import PartitionSpec as P
 
 epsilon = 1e-06
+lag = 2
 MESH = pl.DeviceIdType.MESH
 
 
@@ -41,11 +42,12 @@
 
 
 def scatter_kernel(Z, J, n, sub, with_loss, *refs):
-    if with_loss:
+    if not with_loss:
+        (lhs, w, x, gain, target, wbuf, p, r1, s1, r2, s2, r3, wsem,
+         cs, cr, ys, yr, zs, zr, out, tb, tr, hs, hr) = refs
+    else:
         (lhs, w, part, out, total, wbuf, p, r1, s1, r2, s2, r3, wsem,
          cs, cr, ys, yr, zs, zr, heard, hs, hr) = refs
-    else:
-        (lhs, w, out, wbuf, p, r1, s1, r2, s2, r3, wsem, cs, cr, ys, yr, zs, zr) = refs
     f32 = jnp.float32
     me, c, y, z, core, across, line = position(Z)
     T = 4 * Z
@@ -56,7 +58,7 @@
 
     fetch(0).start()
     others = [lax.rem(me + k, T) for k in range(1, T)]
-    meet(others if with_loss else [core, across] + [v * 4 + y * 2 + c for v in line])
+    meet(others)
     notes = []
     if with_loss:
         for k in range(T - 1):
@@ -73,7 +75,7 @@
         for j in range(J)
     ]
 
-    for t in range(J + 3):
+    for t in range(J + 2 * lag + 1):
         if t < J:
             fetch(t).wait()
             if t + 1 < J:
@@ -98,7 +100,7 @@
             first[j].wait_recv()
             s1[j] = (p[j, :, 1 - y, c].astype(f32) + r1[j, :, 1 - y].astype(f32)).astype(jnp.bfloat16)
             second[j].start()
-        j = t - 2
+        j = t - 1 - lag
         if 0 <= j < J:
             second[j].wait_recv()
             s2[j] = (
@@ -106,13 +108,26 @@
             ).astype(jnp.bfloat16)
             for copy in third[j]:
                 copy.start()
-        j = t - 3
+        j = t - 1 - 2 * lag
         if 0 <= j < J:
             own = p[j, z, y, c].astype(f32) + r1[j, z, y].astype(f32) + r2[j, z].astype(f32)
             for k, copy in enumerate(third[j]):
                 copy.wait_recv()
                 own += r3[j, k].astype(f32)
             out[:, j * n : (j + 1) * n] = own.astype(out.dtype)
+    if not with_loss:
+        whole = out[...]
+        inv_norm = lax.rsqrt(jnp.mean(whole * whole, axis=-1, keepdims=True) + epsilon)
+        size = target.shape[1]
+        for d in range(T):
+            cols = slice(d * size, (d + 1) * size)
+            tb[d] = (
+                x[:, cols].astype(f32) + out[:, cols] * inv_norm * gain[:, cols].astype(f32)
+            ).astype(jnp.bfloat16)
+        for k, v in enumerate(others):
+            notes.append(send(tb.at[v], tr.at[me], hs.at[k], hr.at[k], v))
+            notes[-1].start()
+        tr[me] = tb[me]
     for j in range(J):
         first[j].wait_send()
         second[j].wait_send()
@@ -124,6 +139,10 @@
             copy.wait()
             acc += heard[k]
         total[...] = acc
+    else:
+        for copy in notes:
+            copy.wait()
+        target[...] = tr[...].reshape(target.shape)
 
 
 def gather_kernel(Z, J, n, S, m, G, x, st, gate, up, hidden, student, wbuf, xa, xs, acc,
@@ -194,23 +213,26 @@
             for copy in fetch(j + 2):
                 copy.start()
 
-    for t in range(J + S + 3):
+    for t in range(J + S + 2 * lag + 1):
         if t < J + S:
             for copy in first[t]:
                 copy.start()
-        if 0 <= t - 1 < J + S:
-            for copy in first[t - 1]:
+        i = t - lag
+        if 0 <= i < J + S:
+            for copy in first[i]:
                 copy.wait_recv()
-            second[t - 1].start()
-        if 0 <= t - 2 < J + S:
-            second[t - 2].wait_recv()
-            third[t - 2].start()
-        if 0 <= t - 3 < J + S:
-            third[t - 3].wait_recv()
-            if t - 3 < J:
-                multiply(t - 3)
+            second[i].start()
+        i = t - 2 * lag
+        if 0 <= i < J + S:
+            second[i].wait_recv()
+            third[i].start()
+        i = t - 2 * lag - 1
+        if 0 <= i < J + S:
+            third[i].wait_recv()
+            if i < J:
+                multiply(i)
             else:
-                j = t - 3 - J
+                j = i - J
                 student[:, j * m : (j + 1) * m] = xs[j].reshape(R, m)
     for i in range(J + S):
         for copy in first[i]:
@@ -252,7 +274,7 @@
     )(x, st, gate, up)
 
 
-def scatter_matmul(lhs, w, T, n, sub, dtype, name, cid, part=None):
+def scatter_matmul(lhs, w, T, n, sub, name, cid, part=None, x=None, gain=None):
     Z = T // 4
     rows = lhs.shape[1]
     K, N = w.shape
@@ -267,13 +289,16 @@
         V((J, Z, B, n), bf), V((J, Z, B, n), bf), V((J, Z - 1, B, n), bf), D((2,)),
         D((J,)), D((J,)), D((J,)), D((J,)), D((J, Z - 1)), D((J, Z - 1)),
     ]
-    outs = [jax.ShapeDtypeStruct((B, N), dtype)]
-    args = [lhs, w]
-    specs = [vm, pl.BlockSpec(memory_space=pl.ANY)]
+    specs = [vm, pl.BlockSpec(memory_space=pl.ANY), vm]
     if with_loss:
         scratch += [V((T - 1, 8, 128), jnp.float32), D((T - 1,)), D((T - 1,))]
-        outs.append(jax.ShapeDtypeStruct((8, 128), jnp.float32))
-        args.append(part)
+        outs = [jax.ShapeDtypeStruct((B, N), bf), jax.ShapeDtypeStruct((8, 128), jnp.float32)]
+        args = [lhs, w, part]
+    else:
+        scratch += [V((B, N), jnp.float32), V((T, B, N // T), bf), V((T, B, N // T), bf)]
+        scratch += [D((T - 1,)), D((T - 1,))]
+        outs = [jax.ShapeDtypeStruct((rows, N // T), bf)]
+        args = [lhs, w, x, gain]
         specs.append(vm)
     return pl.pallas_call(
         functools.partial(scatter_kernel, Z, J, n, sub, with_loss),
@@ -294,7 +319,6 @@
 def local(teacher_in, gate_weight, up_weight, down_weight, post_gain, student_in, proj_weight):
     width_count = lax.axis_size("tensor")
     own_sums = width_count == 16 and teacher_in.shape[0] % 16 == 0
-    gains = post_gain.astype(jnp.float32)
     contract_last = (((1,), (1,)), ((), ()))
     if own_sums:
         hidden, student_all = gather_ffn(
@@ -311,8 +335,9 @@
         hidden = (jax.nn.gelu(gate_value, approximate=True) * lift_value).astype(jnp.bfloat16)
         student_all = lax.all_gather(student_in, "tensor", axis=0, tiled=True)
     if own_sums:
-        (ffn_out,) = scatter_matmul(
-            hidden, down_weight, width_count, 768, 256, jnp.float32, "down_scatter", 1
+        (target,) = scatter_matmul(
+            hidden, down_weight, width_count, 384, 384, "down_scatter", 1,
+            x=teacher_in, gain=post_gain[None],
         )
     else:
         ffn_out = lax.psum_scatter(
@@ -321,9 +346,11 @@
             scatter_dimension=0,
             tiled=True,
         )
-    inv_norm = lax.rsqrt(jnp.mean(ffn_out * ffn_out, axis=-1, keepdims=True) + epsilon)
-    target_rows = (teacher_in.astype(jnp.float32) + ffn_out * inv_norm * gains).astype(jnp.bfloat16)
-    target = lax.all_to_all(target_rows, "tensor", split_axis=1, concat_axis=0, tiled=True)
+        inv_norm = lax.rsqrt(jnp.mean(ffn_out * ffn_out, axis=-1, keepdims=True) + epsilon)
+        target_rows = (
+            teacher_in.astype(jnp.float32) + ffn_out * inv_norm * post_gain.astype(jnp.float32)
+        ).astype(jnp.bfloat16)
+        target = lax.all_to_all(target_rows, "tensor", split_axis=1, concat_axis=0, tiled=True)
     projected = lax.dot_general(
         student_all, proj_weight, contract_last, preferred_element_type=jnp.float32
     )
@@ -335,8 +362,8 @@
     )
     if own_sums:
         student_grad, total = scatter_matmul(
-            cotangent[None], proj_weight, width_count, 512, 256, jnp.bfloat16, "grad_scatter", 2,
-            jnp.full((8, 128), squares, jnp.float32),
+            cotangent[None], proj_weight, width_count, 256, 256, "grad_scatter", 2,
+            part=jnp.full((8, 128), squares, jnp.float32),
         )
         total_error = total[0, 0]
     else:

time: 172 us -> 155 us (0.901)
  blocking collectives: 17.7 us -> 0 us
  Pallas kernels: 140 us -> 142 us
    all_to_all x1 -> x0, blocking collectives: 17.7 us -> none  [local(): lax.all_to_all(target_rows, 'tensor', split_axis=1, concat_axis=0, tiled=...]
    pallas_call x2, Pallas kernels: 70.6 us -> 82.1 us  [scatter_matmul(): pl.pallas_call(functools.partial(scatter_kernel, Z, J, n, sub, with_loss)...]
    pallas_call x1, Pallas kernels: 69.8 us -> 60.3 us  [gather_ffn(): pl.pallas_call(functools.partial(gather_kernel, Z, J, n, S, m, G), out_sh...]
where the time goes in v3:
time: 155 us; the launch traced here: 154 us
  Pallas kernels  142 us (92%)
  local copies, waits for them, and re-layouts  4.44 us (3%)
  matrix products  4.37 us (3%)
  between operations  2.48 us (2%)
    pallas_call x2, Pallas kernels, scatter_matmul(): pl.pallas_call(functools.partial(scatter_kernel, Z, J, n, sub, with_loss)...  82.1 us
    pallas_call x1, Pallas kernels, gather_ffn(): pl.pallas_call(functools.partial(gather_kernel, Z, J, n, S, m, G), out_sh...  60.3 us

profile of v3, /device:TPU:0, one launch (start us, length us, event | category | flops | bytes accessed | tf_op | source)
XLA Modules:
  0.0 154.5 jit_solution(13193150848029739134)
XLA Ops:
  0.6 0.7 broadcast_in_dim.9.refs_3_
  1.4 0.0 copy-start.1
  1.4 1.0 copy-done.1
  2.3 0.0 copy-start.2
  2.3 0.9 copy-done.2
  3.3 60.3 %gather_ffn.1 = (bf16[6,512,224]{2,1,0:T(8,128)(2,1)S(1)}, bf16[512,2560]{1,0:T(8,128)(2,1)S(1)}) custom-call(bf16[32,5376]{1,0:T(8,128)(2,1)S(1)} %copy-done.1, bf16[32,2560]{1,0:T(8,128)(2,1)S(1)} %copy-done.2, bf16[1344,5376]{1,0:T(8,128)(2,1)} %gate.1, bf16[1344,5376]{1,0:T(8,128)(2,1)} %up.1), custom_call_target="tpu_custom_call" | custom-call | flops 14797504512 | bytes 28901376 | tf_op jit(solution)/shard_map/gather_ffn/pallas_call | solution.py:254
  63.5 0.0 copy-start
  63.6 51.3 %down_scatter.1 = bf16[512,336]{1,0:T(8,128)(2,1)S(1)} custom-call(bf16[6,512,224]{2,1,0:T(8,128)(2,1)S(1)} %get-tuple-element.8.refs_0_, bf16[1344,5376]{1,0:T(8,128)(2,1)} %refs_1_.2, bf16[32,5376]{1,0:T(8,128)(2,1)S(1)} %copy-done.1, bf16[1,5376]{1,0:T(2,128)(2,1)S(1)} %broadcast_in_dim.9.refs_3_), custom_call_target="tpu_custom_call" | custom-call | flops 7398752256 | bytes 15826944 | tf_op jit(solution)/shard_map/down_scatter/pallas_call | solution.py:303
  114.9 0.0 copy-done
  114.9 1.5 convolution_subtract_fusion
  116.4 0.8 multiply_reduce_fusion
  117.2 0.6 broadcast_in_dim.11.refs_2_
  117.9 30.8 %grad_scatter.1 = (bf16[32,2560]{1,0:T(8,128)(2,1)S(1)}, f32[8,128]{1,0:T(8,128)S(1)}) custom-call(bf16[1,512,336]{2,1,0:T(8,128)(2,1)S(1)} %get-tuple-element.12.refs_0_, bf16[336,2560]{1,0:T(8,128)(2,1)S(1)} %copy-done, f32[8,128]{1,0:T(8,128)S(1)} %broadcast_in_dim.11.refs_2_), custom_call_target="tpu_custom_call" | custom-call | flops 880803840 | bytes 2064384 | tf_op jit(solution)/shard_map/grad_scatter/pallas_call | solution.py:303
  148.7 0.5 slice.3
  149.8 2.8 %fusion = f32[336,2560]{1,0:T(8,128)} fusion(bf16[512,2560]{1,0:T(8,128)(2,1)S(1)} %get-tuple-element.7, f32[512,336]{1,0:T(8,128)S(1)} %convolution_subtract_fusion), kind=kOutput, calls=%fused_computation.2 | convolution fusion | flops 880975872 | bytes 6750208 | tf_op jit(solution)/shard_map/dot_general | solution.py:360
  152.7 0.7 copy.13
Async XLA Ops:
  1.4 1.0 copy-start.1
  2.3 0.9 copy-start.2
  63.5 51.3 %copy-start = (bf16[336,2560]{1,0:T(8,128)(2,1)S(1)}, bf16[336,2560]{1,0:T(8,128)(2,1)}, u32[]{:S(2)}) copy-start(bf16[336,2560]{1,0:T(8,128)(2,1)} %refs_1_.3) | copy-start | bytes 5160964

commit v4 on v3

--- a/solution.py
+++ b/solution.py
@@ -75,7 +75,7 @@
         for j in range(J)
     ]
 
-    for t in range(J + 2 * lag + 1):
+    for t in range(J + 3):
         if t < J:
             fetch(t).wait()
             if t + 1 < J:
@@ -100,7 +100,7 @@
             first[j].wait_recv()
             s1[j] = (p[j, :, 1 - y, c].astype(f32) + r1[j, :, 1 - y].astype(f32)).astype(jnp.bfloat16)
             second[j].start()
-        j = t - 1 - lag
+        j = t - 2
         if 0 <= j < J:
             second[j].wait_recv()
             s2[j] = (
@@ -108,7 +108,7 @@
             ).astype(jnp.bfloat16)
             for copy in third[j]:
                 copy.start()
-        j = t - 1 - 2 * lag
+        j = t - 3
         if 0 <= j < J:
             own = p[j, z, y, c].astype(f32) + r1[j, z, y].astype(f32) + r2[j, z].astype(f32)
             for k, copy in enumerate(third[j]):
@@ -183,7 +183,10 @@
         for i, a in enumerate(items)
     ]
     third = [
-        send(a.at[:, :, c], a.at[:, :, c], cs.at[i], cr.at[i], core)
+        [
+            send(a.at[:, v, c], a.at[:, v, c], cs.at[i, k], cr.at[i, k], core)
+            for k, v in enumerate((y, 1 - y))
+        ]
         for i, a in enumerate(items)
     ]
 
@@ -222,13 +225,15 @@
             for copy in first[i]:
                 copy.wait_recv()
             second[i].start()
+            third[i][0].start()
         i = t - 2 * lag
         if 0 <= i < J + S:
             second[i].wait_recv()
-            third[i].start()
+            third[i][1].start()
         i = t - 2 * lag - 1
         if 0 <= i < J + S:
-            third[i].wait_recv()
+            for copy in third[i]:
+                copy.wait_recv()
             if i < J:
                 multiply(i)
             else:
@@ -238,7 +243,8 @@
         for copy in first[i]:
             copy.wait_send()
         second[i].wait_send()
-        third[i].wait_send()
+        for copy in third[i]:
+            copy.wait_send()
 
 
 def gather_ffn(x, st, gate, up, T, n, m, G, cid):
@@ -262,7 +268,7 @@
         scratch_shapes=[
             V((2, 2, N, n), bf), V((J, Z, 2, 2, B, n), bf), V((S, Z, 2, 2, B, m), bf),
             V((2, G, T * B, N // G), jnp.float32), D((2, 2)),
-            D((J + S, Z - 1)), D((J + S, Z - 1)), D((J + S,)), D((J + S,)), D((J + S,)), D((J + S,)),
+            D((J + S, Z - 1)), D((J + S, Z - 1)), D((J + S,)), D((J + S,)), D((J + S, 2)), D((J + S, 2)),
         ],
         name="gather_ffn",
         cost_estimate=pl.CostEstimate(
@@ -362,7 +368,7 @@
     )
     if own_sums:
         student_grad, total = scatter_matmul(
-            cotangent[None], proj_weight, width_count, 256, 256, "grad_scatter", 2,
+            cotangent[None], proj_weight, width_count, 512, 256, "grad_scatter", 2,
             part=jnp.full((8, 128), squares, jnp.float32),
         )
         total_error = total[0, 0]

time: 155 us -> 168 us (1.084)
  Pallas kernels: 142 us -> 156 us
    pallas_call x2, Pallas kernels: 82.1 us -> 95.6 us  [scatter_matmul(): pl.pallas_call(functools.partial(scatter_kernel, Z, J, n, sub, with_loss)...]
where the time goes in v4:
time: 168 us
  Pallas kernels  156 us (93%)
  local copies, waits for them, and re-layouts  4.44 us (3%)
  matrix products  4.37 us (3%)
  between operations  2.48 us (1%)
    pallas_call x2, Pallas kernels, scatter_matmul(): pl.pallas_call(functools.partial(scatter_kernel, Z, J, n, sub, with_loss)...  95.6 us
    pallas_call x1, Pallas kernels, gather_ffn(): pl.pallas_call(functools.partial(gather_kernel, Z, J, n, S, m, G), out_sh...  60.3 us

profile of v4, /device:TPU:0, one launch (start us, length us, event | category | flops | bytes accessed | tf_op | source)
XLA Modules:
  0.0 168.0 jit_solution(17779574514573132674)
XLA Ops:
  0.6 0.7 broadcast_in_dim.9.refs_3_
  1.4 0.0 copy-start.1
  1.4 1.0 copy-done.1
  2.3 0.0 copy-start.2
  2.3 0.9 copy-done.2
  3.3 60.3 %gather_ffn.1 = (bf16[6,512,224]{2,1,0:T(8,128)(2,1)S(1)}, bf16[512,2560]{1,0:T(8,128)(2,1)S(1)}) custom-call(bf16[32,5376]{1,0:T(8,128)(2,1)S(1)} %copy-done.1, bf16[32,2560]{1,0:T(8,128)(2,1)S(1)} %copy-done.2, bf16[1344,5376]{1,0:T(8,128)(2,1)} %gate.1, bf16[1344,5376]{1,0:T(8,128)(2,1)} %up.1), custom_call_target="tpu_custom_call" | custom-call | flops 14797504512 | bytes 28901376 | tf_op jit(solution)/shard_map/gather_ffn/pallas_call | solution.py:260
  63.5 0.0 copy-start
  63.5 64.6 %down_scatter.1 = bf16[512,336]{1,0:T(8,128)(2,1)S(1)} custom-call(bf16[6,512,224]{2,1,0:T(8,128)(2,1)S(1)} %get-tuple-element.8.refs_0_, bf16[1344,5376]{1,0:T(8,128)(2,1)} %refs_1_.2, bf16[32,5376]{1,0:T(8,128)(2,1)S(1)} %copy-done.1, bf16[1,5376]{1,0:T(2,128)(2,1)S(1)} %broadcast_in_dim.9.refs_3_), custom_call_target="tpu_custom_call" | custom-call | flops 7398752256 | bytes 15826944 | tf_op jit(solution)/shard_map/down_scatter/pallas_call | solution.py:309
  128.1 0.0 copy-done
  128.1 1.5 convolution_subtract_fusion
  129.7 0.8 multiply_reduce_fusion
  130.5 0.6 broadcast_in_dim.11.refs_2_
  131.1 31.0 %grad_scatter.1 = (bf16[32,2560]{1,0:T(8,128)(2,1)S(1)}, f32[8,128]{1,0:T(8,128)S(1)}) custom-call(bf16[1,512,336]{2,1,0:T(8,128)(2,1)S(1)} %get-tuple-element.12.refs_0_, bf16[336,2560]{1,0:T(8,128)(2,1)S(1)} %copy-done, f32[8,128]{1,0:T(8,128)S(1)} %broadcast_in_dim.11.refs_2_), custom_call_target="tpu_custom_call" | custom-call | flops 880803840 | bytes 2064384 | tf_op jit(solution)/shard_map/grad_scatter/pallas_call | solution.py:309
  162.2 0.5 slice.3
  163.3 2.8 %fusion = f32[336,2560]{1,0:T(8,128)} fusion(bf16[512,2560]{1,0:T(8,128)(2,1)S(1)} %get-tuple-element.7, f32[512,336]{1,0:T(8,128)S(1)} %convolution_subtract_fusion), kind=kOutput, calls=%fused_computation.2 | convolution fusion | flops 880975872 | bytes 6750208 | tf_op jit(solution)/shard_map/dot_general | solution.py:366
  166.2 0.7 copy.13
Async XLA Ops:
  1.4 1.0 copy-start.1
  2.3 0.9 copy-start.2
  63.5 64.6 %copy-start = (bf16[336,2560]{1,0:T(8,128)(2,1)S(1)}, bf16[336,2560]{1,0:T(8,128)(2,1)}, u32[]{:S(2)}) copy-start(bf16[336,2560]{1,0:T(8,128)(2,1)} %refs_1_.3) | copy-start | bytes 5160964
